TPU v7x, 768 devices: a whole 4x8x12 slice. The times are simulated.
768 devices in a mesh: prow: 64 (over y, x, core), pcol: 12 (over z).
Axes of the slice: x: 4, y: 8, z: 12, core: 2. Of those that a mesh axis runs over, the one named last changes fastest.
Arguments:
- matrix: float32 [49152, 9216], P('prow', 'pcol'), may hold values from -6 to 6
- panel: float32 [49152, 512], P(('prow', 'pcol')), may hold values from -0.25 to 0.3
- pivot_rows: int32 [512], replicated, may hold values from 0 to 49151, as said below
Outputs:
- factored: float32 [49152, 9216], P('prow', 'pcol')
Inputs may be any that keep to these rules, and one draw needn't show every extreme that they name: `pivot_rows`: the entries are distinct; 0 and 49151 always occur.
All inputs are finite; a program needn't handle non-finite values.
Results may differ from a plain program's by a relative error of at most 0.00005.
Values sent between devices are 32-bit elements; how exact they have to be, the bound alone decides.
A program may use at most 32 MiB of HBM per device.

v0:
```python
import jax
import jax.numpy as jnp
from jax import lax
from jax.sharding import PartitionSpec as P

NB = 512


def from_root(value, axis, source):
    kept = jnp.where(lax.axis_index(axis) == source, value, 0).astype(value.dtype)
    return lax.psum(kept, axis)


def shards(matrix, panel, pivot_rows):
    own_rows = matrix.shape[0]
    own_cols = matrix.shape[1]
    row_base = lax.axis_index("prow") * own_rows
    local_rows = pivot_rows - row_base
    owned = (local_rows >= 0) & (local_rows < own_rows)
    picked = jnp.take(matrix, jnp.clip(local_rows, 0, own_rows - 1), axis=0)
    picked = jnp.where(owned[:, None], picked, 0.0)
    top_pack = jnp.concatenate([matrix[:NB].reshape(-1), panel.reshape(-1)])
    top_pack = from_root(top_pack, "prow", 0)
    split_at = NB * own_cols
    top_rows = top_pack[:split_at].reshape(NB, own_cols)
    lead_panel = top_pack[split_at:].reshape(panel.shape)
    lower_block = lax.all_gather(lead_panel, "pcol", axis=0, tiled=True)[:NB]
    new_top = lax.psum(picked, "prow")
    upper_block = lax.linalg.triangular_solve(
        lower_block, new_top, left_side=True, lower=True, unit_diagonal=True
    )
    vacated = pivot_rows >= NB
    top_index = jnp.arange(NB, dtype=jnp.int32)
    chosen = jnp.any(pivot_rows[None, :] == top_index[:, None], axis=1)
    leftover = jnp.logical_not(chosen)
    left_count = leftover.astype(jnp.int32)
    left_rank = jnp.cumsum(left_count) - left_count
    below = vacated[None, :] & (pivot_rows[None, :] < pivot_rows[:, None])
    vac_rank = jnp.sum(below.astype(jnp.int32), axis=1)
    pairing = leftover[None, :] & (left_rank[None, :] == vac_rank[:, None])
    source_index = jnp.sum(jnp.where(pairing, top_index[None, :], 0), axis=1)
    incoming = jnp.take(top_rows, source_index, axis=0)
    target = jnp.where(vacated & owned, local_rows, own_rows)
    swapped = matrix.at[target].set(incoming, mode="drop")
    product = jnp.dot(
        lax.all_gather(panel, "pcol", axis=0, tiled=True),
        upper_block,
        precision=lax.Precision.HIGHEST,
        preferred_element_type=jnp.float32,
    )
    updated = swapped - product
    global_rows = row_base + jnp.arange(own_rows, dtype=jnp.int32)
    top_fill = jnp.pad(upper_block, ((0, own_rows - NB), (0, 0)))
    return jnp.where((global_rows < NB)[:, None], top_fill, updated)


def solution(mesh):
    return jax.shard_map(
        shards,
        mesh=mesh,
        in_specs=(P("prow", "pcol"), P(("prow", "pcol"), None), P()),
        out_specs=P("prow", "pcol"),
        check_vma=False,
    )
```

profile of v0, /device:TPU:1, one launch (start us, length us, event | category | flops | bytes accessed | tf_op | source)
XLA Modules:
  0.0 371.5 jit_solution(7911866298067007870)
XLA Ops:
  6.5 0.0 copy-start.4
  6.5 0.0 all-reduce.4.cloned.1.call-start
  6.5 1.7 copy.20
  8.2 0.0 copy-done.4
  8.2 1.2 slice.51
  9.5 2.6 gather_fusion
  12.1 0.0 copy-start.2
  12.1 2.5 reshape.91
  14.6 0.0 copy-done.2
  14.6 0.0 copy-start
  14.6 2.9 select_select_fusion
  17.5 0.0 copy-done
  17.5 1.3 maximum_select_fusion
  18.8 0.0 all-reduce.4.cloned.1.call-update
  18.9 0.0 all-gather.3.cloned.1.call-start
  18.9 220.8 %all-reduce.4.cloned.1.call-done = (f32[425984]{0:T(1024)}, f32[512,768]{1,0:T(8,128)}) async-done(((f32[425984]{0:T(1024)}, f32[512,768]{1,0:T(8,128)}), (f32[425984]{0:T(1024)}, f32[512,768]{1,0:T(8,128)})) %all-reduce.4.cloned.1.call-update) | async-done | bytes 3276816 | tf_op jit(solution)/shard_map/psum | solution.py:11
  239.7 0.9 slice.73
  240.7 0.7 slice.53
  241.3 0.0 all-gather.3.cloned.1.call-update
  241.3 0.0 all-gather.5.cloned.1.call-start
  241.4 0.7 all-gather.5.cloned.1.call-update
  242.1 0.2 fusion.9
  242.3 0.3 reduce-window.9
  242.7 0.1 slice.55
  242.8 0.1 slice_reduce_fusion
  242.9 0.1 convert_subtract_fusion
  243.0 0.3 convert_reduce_fusion
  243.2 0.4 select_reduce_fusion
  243.7 2.7 slice.75
  246.3 2.6 reshape.94
  248.9 7.5 %scatter_custom_fusion = f32[768,768]{1,0:T(8,128)S(1)} fusion(f32[768,768]{1,0:T(8,128)S(1)} %copy.20, s32[512]{0:T(512)S(1)} %compare_select_fusion.2, f32[]{:T(128)} %constant.55.clone.1, pred[512]{0:T(512)(128)(4,1)S(1)} %compare_and_fusion, f32[512,768]{1,0:T(8,128)} %reshape.94, s32[1024]{0:T(1024)S(1)} %pad_clamp_fusion), kind=kCustom, calls=%fused_computation.9 | custom fusion | flops 393216 | bytes 3936772 | tf_op jit(solution)/shard_map/scatter | solution.py:44
  256.4 40.2 %all-gather.3.cloned.1.call-done = f32[768,512]{1,0:T(8,128)} async-done(((f32[64,512]{1,0:T(8,128)}), f32[768,512]{1,0:T(8,128)}) %all-gather.3.cloned.1.call-update) | async-done | bytes 1572880 | tf_op jit(solution)/shard_map/all_gather | solution.py:27
  296.6 1.4 fusion.8
  298.0 10.9 %while.1 = (s32[]{:T(128)}, f32[512,512]{1,0:T(8,128)S(1)}, s32[4,2]{0,1:T(2,128)S(1)}, f32[4,128,128]{2,1,0:T(8,128)}, s32[]{:T(128)}) while((s32[]{:T(128)}, f32[512,512]{1,0:T(8,128)S(1)}, s32[4,2]{0,1:T(2,128)S(1)}, f32[4,128,128]{2,1,0:T(8,128)}, s32[]{:T(128)}) %tuple.23), condition=%wide.while_cond, body=%wide.while_body.sunk | while | flops 2 | bytes 132705 | solution.py:29
  298.0 0.1 constant_dynamic-slice_fusion.2
  298.1 0.6 fusion.35
  298.7 2.0 bitcast_dynamic-update-slice_fusion.2
  300.7 0.1 constant_dynamic-slice_fusion.2
  300.8 0.6 fusion.35
  301.4 2.0 bitcast_dynamic-update-slice_fusion.2
  303.5 0.1 constant_dynamic-slice_fusion.2
  303.5 0.6 fusion.35
  304.1 2.0 bitcast_dynamic-update-slice_fusion.2
  306.2 0.1 constant_dynamic-slice_fusion.2
  306.2 0.6 fusion.35
  306.8 2.0 bitcast_dynamic-update-slice_fusion.2
  308.9 40.8 %custom-call.3 = f32[4,128,128]{1,2,0:T(8,128)} custom-call(f32[4,128,128]{2,1,0:T(8,128)} %get-tuple-element.12), custom_call_target="InvertDiagBlocksLowerTriangular" | custom-call | tf_op jit(solution)/shard_map/triangular_solve | solution.py:29
  349.6 0.0 copy-start.3
  349.6 0.0 copy-start.1
  349.6 1.7 fusion.15
  351.3 1.5 convolution_subtract_fusion.1
  352.8 0.0 copy-done.3
  352.8 0.5 fusion.22
  353.3 0.0 copy-done.1
  353.3 0.6 convolution_subtract_fusion.2
  353.9 0.5 fusion.20
  354.4 0.9 convolution_subtract_fusion
  355.3 0.5 fusion.19
  355.9 1.3 pad_maximum_fusion
  357.1 0.0 all-gather.5.cloned.1.call-done
  357.1 7.8 %fusion = f32[768,768]{1,0:T(8,128)} fusion(f32[768,768]{1,0:T(8,128)S(1)} %scatter_custom_fusion, f32[512,768]{1,0:T(8,128)} %pad_maximum_fusion, f32[768,512]{1,0:T(8,128)} %all-gather.5.cloned.1.call-done, pred[768]{0:T(1024)(128)(4,1)S(1)} %add_compare_fusion), kind=kOutput, calls=%fused_computation.6 | convolution fusion | flops 3625058304 | bytes 7865088 | tf_op jit(solution)/shard_map/dot_general | solution.py:45
  (14 shorter events, 0.1 us)
Async XLA Ops:
  6.5 1.7 copy-start.4
  6.5 233.2 %all-reduce.4.cloned.1.call-start = ((), (), s32[]{:S(2)}) async-start(), calls=%async_computation.2 | async-start | bytes 6553600 | tf_op jit(solution)/shard_map/psum | solution.py:11
  12.1 2.5 copy-start.2
  14.6 2.9 copy-start
  18.9 277.7 %all-gather.3.cloned.1.call-start = ((), (), s32[]{:S(2)}) async-start(), calls=%async_computation | async-start | bytes 1703936 | tf_op jit(solution)/shard_map/all_gather | solution.py:27
  241.3 115.8 %all-gather.5.cloned.1.call-start = ((), (), s32[]{:S(2)}) async-start(), calls=%async_computation.1 | async-start | bytes 1703936 | tf_op jit(solution)/shard_map/all_gather | solution.py:46
  349.6 3.2 copy-start.3
  349.6 3.7 copy-start.1
Sparse Core Ops, SparseCore 0:
  19.0 220.6 all-reduce.3
  242.1 54.4 all-gather.2
  299.0 57.3 all-gather.4
where the time goes:
time: 378 us; the launch traced here: 371 us
  waiting for transfers between devices  262 us (69%)
  other arithmetic  56.4 us (15%)
  local copies, waits for them, and re-layouts  25.9 us (7%)
  matrix products  14 us (4%)
  between operations  13.3 us (4%)
    psum x1, waiting for transfers between devices, from_root(): return lax.psum(kept, axis)  221 us
    another operation x5, other arithmetic, shards(): lax.linalg.triangular_solve(lower_block, new_top, left_side=True, lower=T...  43.4 us
    all_gather x1, waiting for transfers between devices, shards(): lower_block = lax.all_gather(lead_panel, 'pcol', axis=0, tiled=True)[:NB]  40.2 us
    another operation x14, local copies, waits for them, and re-layouts  11 us
    dot_general x1, matrix products, shards(): jnp.dot(lax.all_gather(panel, 'pcol', axis=0, tiled=True), upper_block, p...  7.84 us
  transfers between devices with their start and end apart: 3, of which 2 were waited for; matrix products, arithmetic and copies ran while one was open for 20% of the time, Pallas kernels for 0%

commit v1 on v0

v1 whole, which is shorter than its diff:
```python
import functools

import jax
import jax.numpy as jnp
from jax import lax
from jax.experimental import pallas as pl
from jax.experimental.pallas import tpu as pltpu
from jax.sharding import PartitionSpec as P

NB = 512
NX, NY, NZ = 4, 8, 12
CHIPS = NX * NY
CAP = 32
MESH = pl.DeviceIdType.MESH
F32, BF16, I32 = jnp.float32, jnp.bfloat16, jnp.int32
HIGHEST = lax.Precision.HIGHEST


def mm(a, b, dims=((1,), (0,))):
    return lax.dot_general(a, b, (dims, ((), ())), preferred_element_type=F32)


def split3(v):
    hi = v.astype(BF16)
    rest = v - hi.astype(F32)
    mid = rest.astype(BF16)
    low = (rest - mid.astype(F32)).astype(BF16)
    return hi, mid, low


def select_rows(onehot, v, dims=((1,), (0,))):
    hi, mid, low = split3(v)
    return (mm(onehot, low, dims) + mm(onehot, mid, dims)) + mm(onehot, hi, dims)


def iota(shape, axis):
    return lax.broadcasted_iota(I32, shape, axis)


def chip_of(rows):
    return ((rows >> 9) * 171) >> 9


def count(mask, axis):
    return jnp.sum(mask.astype(F32), axis=axis, keepdims=True).astype(I32)


def prep_kernel(me_ref, prow_ref, pcol_ref, m_ref,
                contrib_ref, sel_ref, dest_ref, ok_ref, top_ref):
    me = me_ref[0]
    rows = m_ref.shape[0]
    half = m_ref.shape[1] // 2
    p_r = prow_ref[...]
    p_c = jnp.broadcast_to(pcol_ref[...], (NB, NB))
    c_r, c_c = chip_of(p_r), chip_of(p_c)
    i0, i1 = iota((NB, NB), 0), iota((NB, NB), 1)
    same = c_c == c_r
    slot_r = count(same & (i0 < i1), 0)
    slot_c = count(same & (i1 < i0), 1)
    d_r = c_r * CAP + slot_r
    dest_ref[...] = jnp.broadcast_to(c_c[:, :1] * CAP + slot_c, dest_ref.shape)
    ok_ref[...] = jnp.broadcast_to(jnp.max(slot_r, axis=1, keepdims=True), ok_ref.shape)
    mine = d_r == (me >> 1) * CAP + iota((CAP, NB), 0)
    row = jnp.sum(jnp.where(mine, (p_r + 1).astype(F32), 0.0), axis=1, keepdims=True).astype(I32) - 1
    pick = (row - me * rows) == iota((CAP, rows), 1)
    got = select_rows(pick.astype(BF16), m_ref[...])
    contrib_ref[0] = got[:, :half]
    contrib_ref[1] = got[:, half:]
    sel_ref[...] = (pick & (row >= NB)).astype(F32)

    @pl.when(me == 0)
    def _():
        t_r = iota((1, NB), 1)
        left_rank = t_r - count(p_c < t_r, 0)
        chosen = count(p_c == t_r, 0) > 0
        left_key = jnp.where(chosen, -2, left_rank)
        vac_rank = count((p_c >= NB) & (p_c < p_r), 0)
        vac_key = jnp.where(p_r >= NB, vac_rank + 1, 0).astype(F32)
        parts = split3(m_ref[:NB])

        @pl.loop(0, CHIPS // 8)
        def _(g):
            rows_at = 8 * CAP
            e = d_r == g * rows_at + iota((rows_at, NB), 0)
            key = jnp.sum(jnp.where(e, vac_key, 0.0), axis=1, keepdims=True).astype(I32) - 1
            onehot = (key == left_key).astype(BF16)
            out = (mm(onehot, parts[2]) + mm(onehot, parts[1])) + mm(onehot, parts[0])
            top_ref[pl.ds(g * 8, 8), 0] = out[:, :half].reshape(8, CAP, half)
            top_ref[pl.ds(g * 8, 8), 1] = out[:, half:].reshape(8, CAP, half)


def prep(me, p_row, p_col, matrix):
    half = matrix.shape[1] // 2
    vm = pl.BlockSpec(memory_space=pltpu.VMEM)
    return pl.pallas_call(
        prep_kernel,
        out_shape=(
            jax.ShapeDtypeStruct((2, CAP, half), F32),
            jax.ShapeDtypeStruct((CAP, matrix.shape[0]), F32),
            jax.ShapeDtypeStruct((NB, 128), I32),
            jax.ShapeDtypeStruct((8, 128), I32),
            jax.ShapeDtypeStruct((CHIPS, 2, CAP, half), F32),
        ),
        in_specs=[pl.BlockSpec(memory_space=pltpu.SMEM), vm, vm, vm],
        out_specs=(vm,) * 5,
        name="prep",
    )(me, p_row, p_col, matrix)


class Ring:
    def __init__(self, n, me, piece, device, send, recv):
        self.n, self.me, self.piece, self.device = n, me, piece, device
        self.send, self.recv = send, recv
        self.waited = set()

    def moves(self, s):
        last = s == self.n // 2 - 1
        return [(d, h) for h in (0, 1) for d in (0, 1) if not (last and d != h)]

    def copy(self, s, d, h, block):
        n = self.n
        ref = self.piece(lax.rem(block + 2 * n, n), h)
        peer = lax.rem(self.me + (1 if d == 0 else n - 1), n)
        return pltpu.make_async_remote_copy(
            src_ref=ref, dst_ref=ref,
            send_sem=self.send.at[d, s, h], recv_sem=self.recv.at[d, s, h],
            device_id=self.device(peer), device_id_type=MESH)

    def out(self, s, d, h):
        return self.copy(s, d, h, self.me - s if d == 0 else self.me + s)

    def arrive(self, s, d, h):
        block = self.me - 1 - s if d == 0 else self.me + 1 + s
        self.copy(s, d, h, block).wait_recv()
        self.waited.add((s, d, h))
        return lax.rem(block + 2 * self.n, self.n)

    def step(self, s, hook=None):
        for d, h in self.moves(s):
            if s > 0:
                block = self.arrive(s - 1, d, h)
                if hook is not None:
                    hook(block, h)
            self.out(s, d, h).start()

    def finish(self, hook=None):
        for s in range(self.n // 2):
            for d, h in self.moves(s):
                if (s, d, h) not in self.waited:
                    block = self.arrive(s, d, h)
                    if hook is not None:
                        hook(block, h)

    def drain(self):
        for s in range(self.n // 2):
            for d, h in self.moves(s):
                self.out(s, d, h).wait_send()


def exchange_kernel(panel_ref, contrib_ref, top_ref,
                    pall_ref, slots_ref, low_ref, tops_ref,
                    from_pair, own, low_in,
                    z_send, z_recv, r_send, r_recv, q_send, q_recv,
                    one_send, one_recv, lone_send, lone_recv,
                    zl_send, zl_recv, sc_send, sc_recv, local,
                    pair_send, pair_recv, slot_send, slot_recv,
                    lpair_send, lpair_recv, top_send, top_recv, tp_send, tp_recv):
    pr = lax.axis_index("prow")
    z = lax.axis_index("pcol")
    core = lax.rem(pr, 2)
    chip = pr // 2
    x = lax.rem(chip, NX)
    y = chip // NX
    half = own.shape[1]

    def dev(x=x, y=y, c=core, z=z):
        return ((y * NX + x) * 2 + c, z)

    def remote(src, dst, ss, rs, device):
        return pltpu.make_async_remote_copy(
            src_ref=src, dst_ref=dst, send_sem=ss, recv_sem=rs,
            device_id=device, device_id_type=MESH)

    partner = dev(c=1 - core)
    is_root = pr == 0
    barrier = pltpu.get_barrier_semaphore()

    def hello(device):
        pl.semaphore_signal(barrier, inc=1, device_id=device, device_id_type=MESH)

    for d in range(1, NZ):
        hello(dev(z=lax.rem(z + d, NZ)))
    for d in range(1, NX):
        hello(dev(x=lax.rem(x + d, NX)))
    for d in range(1, NY):
        hello(dev(y=lax.rem(y + d, NY)))
    hello(partner)
    near = NZ + NX + NY - 2

    @pl.when(is_root)
    def _():
        @pl.loop(1, 2 * CHIPS)
        def _(q):
            hello((q, z))
        pl.semaphore_wait(barrier, near + 2 * CHIPS - 1)

    @pl.when(jnp.logical_not(is_root))
    def _():
        hello((0, z))
        pl.semaphore_wait(barrier, near + 1)

    pltpu.make_async_copy(panel_ref, pall_ref.at[z], local.at[0]).start()
    pltpu.make_async_copy(panel_ref, pall_ref.at[z], local.at[0]).wait()

    def line(mine):
        other = 1 - mine
        n1, n2 = (NX, NY) if mine == 0 else (NY, NX)
        a1, a2 = (x, y) if mine == 0 else (y, x)
        peer1 = (lambda i: dev(x=i)) if mine == 0 else (lambda i: dev(y=i))
        peer2 = (lambda i: dev(y=i)) if mine == 0 else (lambda i: dev(x=i))
        slots = slots_ref.at[mine]
        lows = low_ref.at[mine]

        def part(ref):
            if mine == 0:
                return lambda b, h: ref.at[b, pl.ds(2 * h, 2)]
            return lambda b, h: ref.at[pl.ds(4 * h, 4), b]

        def whole(ref, b):
            return ref.at[b] if mine == 0 else ref.at[:, b]

        zr = Ring(NZ, z, lambda b, h: pall_ref.at[b, pl.ds(32 * h, 32)],
                  lambda i: dev(z=i), z_send, z_recv)
        has_low = (z < NB // 64) & (lax.rem(z, 2) == mine)
        zr.step(0)

        @pl.when(is_root & (z < NB // 64))
        def _():
            @pl.loop(0, CHIPS)
            def _(q):
                src = panel_ref.at[pl.ds(pl.multiple_of(q // NX * 8, 8), 8),
                                   pl.ds(pl.multiple_of(lax.rem(q, NX) * 128, 128), 128)]

                @pl.when((q > 0) | (lax.rem(z, 2) == 1))
                def _():
                    remote(src, low_in, sc_send.at[q], sc_recv,
                           (q * 2 + lax.rem(z, 2), z)).start()

        @pl.when(is_root & has_low)
        def _():
            pltpu.make_async_copy(panel_ref.at[pl.ds(0, 8), pl.ds(0, 128)], low_in, local.at[1]).start()
            pltpu.make_async_copy(panel_ref.at[pl.ds(0, 8), pl.ds(0, 128)], low_in, local.at[1]).wait()

        pair = remote(contrib_ref.at[other], from_pair, pair_send, pair_recv, partner)
        pair.start()

        @pl.when(is_root)
        def _():
            remote(top_ref.at[0, 1], tops_ref.at[1], tp_send.at[1], top_recv, partner).start()

            @pl.loop(1, CHIPS)
            def _(q):
                for c in (0, 1):
                    remote(top_ref.at[q, c], tops_ref.at[c], top_send, top_recv, (q * 2 + c, z)).start()

        pair.wait_recv()
        own[...] = contrib_ref[mine] + from_pair[...]
        keep = pltpu.make_async_copy(own, slots.at[y, x], local.at[2])
        keep.start()
        first = []
        for d in range(1, n1):
            first.append(remote(own, slots.at[y, x], one_send.at[d], one_recv.at[d],
                                peer1(lax.rem(a1 + d, n1))))
            first[-1].start()
        zr.step(1)

        @pl.when(has_low)
        def _():
            @pl.when(jnp.logical_not(is_root & (mine == 0)))
            def _():
                remote(low_in, low_in, sc_send.at[0], sc_recv, partner).wait_recv()
            pltpu.make_async_copy(low_in, lows.at[y, x, z // 2], local.at[3]).start()
            for d in range(1, NZ):
                remote(low_in, lows.at[y, x, z // 2], zl_send.at[d], zl_recv.at[z // 2],
                       dev(z=lax.rem(z + d, NZ))).start()

        zr.step(2)
        keep.wait()
        for d in range(1, n1):
            src = lax.rem(a1 + n1 - d, n1)
            dst = slots.at[y, src] if mine == 0 else slots.at[src, x]
            remote(dst, dst, one_send.at[d], one_recv.at[d], peer1(src)).wait_recv()
        ring = Ring(n2, a2, part(slots), peer2, r_send, r_recv)
        ring.step(0)

        def to_pair(block, h):
            remote(part(slots)(block, h), part(slots)(block, h), slot_send, slot_recv, partner).start()

        def first_pair():
            for h in (0, 1):
                to_pair(a2, h)

        first_pair()
        zr.step(3)
        for i in range(4):
            @pl.when(z != 2 * i + mine)
            def _():
                ref = lows.at[y, x, i]
                remote(ref, ref, zl_send.at[1], zl_recv.at[i], partner).wait_recv()

        @pl.when(has_low)
        def _():
            pltpu.make_async_copy(low_in, lows.at[y, x, z // 2], local.at[3]).wait()
        lfirst = []
        for d in range(1, n1):
            lfirst.append(remote(lows.at[y, x], lows.at[y, x], lone_send.at[d], lone_recv.at[d],
                                 peer1(lax.rem(a1 + d, n1))))
            lfirst[-1].start()
        ring.step(1, to_pair)
        zr.step(4)
        for d in range(1, n1):
            src = lax.rem(a1 + n1 - d, n1)
            dst = lows.at[y, src] if mine == 0 else lows.at[src, x]
            remote(dst, dst, lone_send.at[d], lone_recv.at[d], peer1(src)).wait_recv()
        lring = Ring(n2, a2, part(lows), peer2, q_send, q_recv)
        lring.step(0)
        for s in range(2, n2 // 2):
            ring.step(s, to_pair)
            if s == 2:
                zr.step(5)
            lring.step(s - 1)
        if n2 // 2 <= 2:
            zr.step(5)
        lring.step(n2 // 2 - 1)
        ring.finish(to_pair)
        lring.finish()
        lpair = remote(lows, lows, lpair_send, lpair_recv, partner)
        lpair.start()

        @pl.when(jnp.logical_not(is_root & (mine == 0)))
        def _():
            remote(tops_ref.at[mine], tops_ref.at[mine], top_send, top_recv, partner).wait_recv()

        @pl.when(is_root & (mine == 0))
        def _():
            pltpu.make_async_copy(top_ref.at[0, 0], tops_ref.at[0], local.at[4]).start()
            pltpu.make_async_copy(top_ref.at[0, 0], tops_ref.at[0], local.at[4]).wait()
        tpair = remote(tops_ref.at[mine], tops_ref.at[mine], tp_send.at[0], tp_recv, partner)
        tpair.start()

        zr.finish()
        remote(slots_ref.at[other], slots_ref.at[other], slot_send, slot_recv, partner).wait_recv()
        remote(low_ref.at[other], low_ref.at[other], lpair_send, lpair_recv, partner).wait_recv()
        remote(tops_ref.at[other], tops_ref.at[other], tp_send.at[0], tp_recv, partner).wait_recv()

        pair.wait_send()
        for c in first + lfirst + [lpair, tpair]:
            c.wait_send()
        ring.drain()
        lring.drain()
        zr.drain()
        remote(slots, slots, slot_send, slot_recv, partner).wait_send()

        @pl.when(has_low)
        def _():
            for d in range(1, NZ):
                remote(low_in, lows.at[y, x, z // 2], zl_send.at[d], zl_recv.at[z // 2],
                       dev(z=lax.rem(z + d, NZ))).wait_send()

        @pl.when(is_root & (z < NB // 64))
        def _():
            @pl.loop(0, CHIPS)
            def _(q):
                @pl.when((q > 0) | (lax.rem(z, 2) == 1))
                def _():
                    remote(low_in, low_in, sc_send.at[q], sc_recv, partner).wait_send()

        @pl.when(is_root)
        def _():
            remote(top_ref.at[0, 1], tops_ref.at[1], tp_send.at[1], top_recv, partner).wait_send()
            rest = top_ref.at[pl.ds(1, CHIPS - 1)]
            remote(rest, rest, top_send, top_recv, partner).wait_send()

    for mine in (0, 1):
        @pl.when(core == mine)
        def _(mine=mine):
            line(mine)


def exchange(panel, contrib, tops):
    half = contrib.shape[2]
    dma = pltpu.SemaphoreType.DMA
    anyspec = pl.BlockSpec(memory_space=pl.ANY)
    vm = pl.BlockSpec(memory_space=pltpu.VMEM)
    return pl.pallas_call(
        exchange_kernel,
        out_shape=(
            jax.ShapeDtypeStruct((NZ,) + panel.shape, F32),
            jax.ShapeDtypeStruct((2, NY, NX, CAP, half), F32),
            jax.ShapeDtypeStruct((2, NY, NX, 4, 8, 128), F32),
            jax.ShapeDtypeStruct((2, CAP, half), F32),
        ),
        in_specs=[vm, vm, anyspec],
        out_specs=(anyspec,) * 4,
        scratch_shapes=[
            pltpu.VMEM((CAP, half), F32),
            pltpu.VMEM((CAP, half), F32),
            pltpu.VMEM((8, 128), F32),
            dma((2, NZ // 2, 2)), dma((2, NZ // 2, 2)),
            dma((2, NY // 2, 2)), dma((2, NY // 2, 2)),
            dma((2, NY // 2, 2)), dma((2, NY // 2, 2)),
            dma((NY,)), dma((NY,)), dma((NY,)), dma((NY,)),
            dma((NZ,)), dma((4,)), dma((CHIPS,)), dma, dma((5,)),
            dma, dma, dma, dma, dma, dma, dma, dma, dma((2,)), dma,
        ],
        compiler_params=pltpu.CompilerParams(collective_id=0, has_side_effects=True),
        name="exchange",
    )(panel, contrib, tops)


def finish_kernel(me_ref, m_ref, pall_ref, slots_ref, low_ref, tops_ref, sel_ref, dest_ref,
                  out_ref, lower, inverse, p_hi, p_lo, perm):
    me = me_ref[0]
    rows = m_ref.shape[0]

    @pl.when(pl.program_id(0) == 0)
    def _():
        for i in range(NB // 64):
            for yy in range(NY):
                for xx in range(NX):
                    if 128 * xx < 64 * i + 64:
                        lower[64 * i + 8 * yy:64 * i + 8 * yy + 8, 128 * xx:128 * xx + 128] = (
                            low_ref[i % 2, yy, xx, i // 2])
        i0, i1 = iota((128, 128), 0), iota((128, 128), 1)
        eye = (i0 == i1).astype(F32)
        diag = [lower[128 * k:128 * k + 128, 128 * k:128 * k + 128] for k in range(4)]
        size = 1
        invs = [eye] * 4
        while size < 128:
            mask = ((i0 // (2 * size)) == (i1 // (2 * size))) & (
                (i0 // size) % 2 == 1) & ((i1 // size) % 2 == 0)
            offs = [jnp.where(mask, d, 0.0) for d in diag]
            if size == 1:
                invs = [eye - o for o in offs]
            else:
                mids = [jnp.dot(o, v, precision=HIGHEST, preferred_element_type=F32)
                        for o, v in zip(offs, invs)]
                invs = [v - jnp.dot(v, t, precision=HIGHEST, preferred_element_type=F32)
                        for v, t in zip(invs, mids)]
            size *= 2
        for k in range(4):
            inverse[k] = invs[k]
        full = pall_ref[...]
        hi = full.astype(BF16)
        p_hi[...] = hi
        p_lo[...] = (full - hi.astype(F32)).astype(BF16)
        for k in range(CHIPS * CAP // 128):
            perm[:, 128 * k:128 * k + 128] = (
                dest_ref[...] == iota((NB, 128), 1) + 128 * k).astype(BF16)

    top = select_rows(perm[...], slots_ref[0])
    done = []
    for i in range(4):
        rhs = top[128 * i:128 * i + 128]
        if i:
            rhs = rhs - jnp.dot(lower[128 * i:128 * i + 128, :128 * i],
                                jnp.concatenate(done, axis=0) if i > 1 else done[0],
                                precision=HIGHEST, preferred_element_type=F32)
        done.append(jnp.dot(inverse[i], rhs, precision=HIGHEST, preferred_element_type=F32))
    upper = jnp.concatenate(done, axis=0)
    u_hi = upper.astype(BF16)
    u_lo = (upper - u_hi.astype(F32)).astype(BF16)
    product = (mm(p_lo[...], u_hi) + mm(p_hi[...], u_lo)) + mm(p_hi[...], u_hi)
    sel = sel_ref[...].astype(BF16)
    incoming = select_rows(sel, tops_ref[0], ((0,), (0,)))
    replaced = mm(sel, jnp.ones((CAP, 128), BF16), ((0,), (0,)))[:, :1] > 0.5
    out_ref[...] = jnp.where(replaced, incoming, m_ref[...]) - product

    @pl.when(me == 0)
    def _():
        out_ref[:NB] = upper


def finish(me, matrix, pall, slots, low, tops, sel, dest):
    rows, cols = matrix.shape
    half = cols // 2
    whole = lambda shape: pl.BlockSpec(shape, lambda n: (0,) * len(shape))
    return pl.pallas_call(
        finish_kernel,
        grid=(2,),
        out_shape=jax.ShapeDtypeStruct(matrix.shape, F32),
        in_specs=[
            pl.BlockSpec(memory_space=pltpu.SMEM),
            pl.BlockSpec((rows, half), lambda n: (0, n)),
            whole((rows, NB)),
            pl.BlockSpec((1, CHIPS * CAP, half), lambda n: (n, 0, 0)),
            whole(low.shape),
            pl.BlockSpec((1, CAP, half), lambda n: (n, 0, 0)),
            whole(sel.shape),
            whole(dest.shape),
        ],
        out_specs=pl.BlockSpec((rows, half), lambda n: (0, n)),
        scratch_shapes=[
            pltpu.VMEM((NB, NB), F32),
            pltpu.VMEM((4, 128, 128), F32),
            pltpu.VMEM((rows, NB), BF16),
            pltpu.VMEM((rows, NB), BF16),
            pltpu.VMEM((NB, CHIPS * CAP), BF16),
        ],
        name="finish",
    )(me, matrix, pall.reshape(rows, NB), slots.reshape(2, CHIPS * CAP, half), low, tops, sel, dest)


def ring_sum(value, axis):
    n = lax.axis_size(axis)
    pairs = [(i, (i + 1) % n) for i in range(n)]

    def body(_, carry):
        total, moving = carry
        moving = lax.ppermute(moving, axis, pairs)
        return total + moving, moving

    return lax.fori_loop(0, n - 1, body, (value, value))[0]


def dense(matrix, panel, pivot_rows):
    own_rows = matrix.shape[0]
    row = lax.axis_index("prow")
    col = lax.axis_index("pcol")
    row_base = row * own_rows
    slab = jnp.zeros((lax.axis_size("pcol"),) + panel.shape, F32)
    panels = ring_sum(lax.dynamic_update_slice(slab, panel[None], (col, 0, 0)), "pcol")
    panels = panels.reshape(own_rows, NB)
    local_rows = pivot_rows - row_base
    owned = (local_rows >= 0) & (local_rows < own_rows)
    picked = (local_rows[:, None] == jnp.arange(own_rows, dtype=I32)[None, :]).astype(F32)
    picked = jnp.dot(picked, matrix, precision=HIGHEST, preferred_element_type=F32)
    first = jnp.where(row == 0, 1.0, 0.0)
    pack = jnp.concatenate([picked, matrix[:NB] * first], axis=1)
    pack = jnp.concatenate([pack, panels[:NB] * first], axis=1)
    pack = ring_sum(pack, "prow")
    own_cols = matrix.shape[1]
    new_top, top_rows, lower = pack[:, :own_cols], pack[:, own_cols:2 * own_cols], pack[:, 2 * own_cols:]

    def solve_row(j, upper):
        coef = lax.dynamic_slice(lower, (j, 0), (1, NB))
        coef = jnp.where(jnp.arange(NB)[None, :] < j, coef, 0.0)
        done = jnp.dot(coef, upper, precision=HIGHEST, preferred_element_type=F32)
        mine = lax.dynamic_slice(upper, (j, 0), (1, own_cols)) - done
        return lax.dynamic_update_slice(upper, mine, (j, 0))

    upper = lax.fori_loop(0, NB, solve_row, new_top)
    vacated = pivot_rows >= NB
    top_index = jnp.arange(NB, dtype=I32)
    chosen = jnp.any(pivot_rows[None, :] == top_index[:, None], axis=1)
    left_rank = top_index - jnp.sum((pivot_rows[None, :] < top_index[:, None]).astype(I32), axis=1)
    vac_rank = jnp.sum((vacated[None, :] & (pivot_rows[None, :] < pivot_rows[:, None])).astype(I32), axis=1)
    pairing = (vacated[:, None] & jnp.logical_not(chosen)[None, :]
               & (left_rank[None, :] == vac_rank[:, None])).astype(F32)
    incoming = jnp.dot(pairing, top_rows, precision=HIGHEST, preferred_element_type=F32)
    global_rows = row_base + jnp.arange(own_rows, dtype=I32)
    place = (global_rows[:, None] == pivot_rows[None, :]) & vacated[None, :]
    moved = jnp.dot(place.astype(F32), incoming, precision=HIGHEST, preferred_element_type=F32)
    swapped = jnp.where(jnp.any(place, axis=1)[:, None], moved, matrix)
    updated = swapped - jnp.dot(panels, upper, precision=HIGHEST, preferred_element_type=F32)
    top_fill = jnp.pad(upper, ((0, own_rows - NB), (0, 0)))
    return jnp.where((global_rows < NB)[:, None], top_fill, updated)


def shards(matrix, panel, pivot_rows):
    me = lax.axis_index("prow").reshape(1)
    contrib, sel, dest, most, tops = prep(me, pivot_rows.reshape(1, NB), pivot_rows.reshape(NB, 1), matrix)

    def fast(_):
        pall, slots, low, top = exchange(panel, contrib, tops)
        return finish(me, matrix, pall, slots, low, top, sel, dest)

    def slow(_):
        return dense(matrix, panel, pivot_rows)

    return lax.cond(most[0, 0] < CAP, fast, slow, 0)


def solution(mesh):
    return jax.shard_map(
        shards,
        mesh=mesh,
        in_specs=(P("prow", "pcol"), P(("prow", "pcol"), None), P()),
        out_specs=P("prow", "pcol"),
        check_vma=False,
    )
```

time: 378 us -> 98.9 us (0.26); the launches traced: 371 us -> 98.7 us
  waiting for transfers between devices: 262 us -> 0 us
  Pallas kernels: 0 us -> 94.9 us
  other arithmetic: 56.4 us -> 0 us
  local copies, waits for them, and re-layouts: 25.9 us -> 2.8 us
  matrix products: 14 us -> 0 us
  between operations: 13.3 us -> 0.67 us
    psum x1 -> x0, waiting for transfers between devices: 221 us -> none  [from_root(): return lax.psum(kept, axis)]
    pallas_call x0 -> x3, Pallas kernels: none -> 94.9 us  [the longest x1 70.6 us: exchange(): pl.pallas_call(exchange_kernel, out_shape=(jax.ShapeDtypeStruct((NZ,) + p...]
    another operation x7 -> x0, other arithmetic: 43.8 us -> none  [the longest x5 43.4 us: shards(): lax.linalg.triangular_solve(lower_block, new_top, left_side=True, lower=T...]
    all_gather x2 -> x0, waiting for transfers between devices: 40.2 us -> none  [the longest x1 40.2 us: shards(): lower_block = lax.all_gather(lead_panel, 'pcol', axis=0, tiled=True)[:NB]]
    another operation x15 -> x0, local copies, waits for them, and re-layouts: 11 us -> none
    dot_general x1 -> x0, matrix products: 7.84 us -> none  [shards(): jnp.dot(lax.all_gather(panel, 'pcol', axis=0, tiled=True), upper_block, p...]
    scatter x1 -> x0, other arithmetic: 7.49 us -> none  [shards(): swapped = matrix.at[target].set(incoming, mode='drop')]
    another operation x7 -> x0, matrix products: 6.15 us -> none  [shards(): lax.linalg.triangular_solve(lower_block, new_top, left_side=True, lower=T...]
  transfers between devices with their start and end apart: 3 -> 0, of which waited for: 2 -> 0; matrix products, arithmetic and copies ran while one was open for 20% -> 0% of each run, Pallas kernels for 0% -> 0%
where the time goes in v1:
time: 98.9 us; the launch traced here: 98.7 us
  Pallas kernels  94.9 us (96%)
  local copies, waits for them, and re-layouts  2.8 us (3%)
    pallas_call x1, Pallas kernels, exchange(): pl.pallas_call(exchange_kernel, out_shape=(jax.ShapeDtypeStruct((NZ,) + p...  70.6 us
    pallas_call x1, Pallas kernels, finish(): pl.pallas_call(finish_kernel, grid=(2,), out_shape=jax.ShapeDtypeStruct(m...  19.7 us
    pallas_call x1, Pallas kernels, prep(): pl.pallas_call(prep_kernel, out_shape=(jax.ShapeDtypeStruct((2, CAP, half...  4.65 us

profile of v1, /device:TPU:1, one launch (start us, length us, event | category | flops | bytes accessed | tf_op | source)
XLA Modules:
  0.0 98.7 jit_solution(2644527373331934981)
XLA Ops:
  0.0 0.0 copy-start.6
  0.0 0.0 copy-start.5
  0.0 1.6 %copy.7.pcol_ref = s32[512,1]{1,0:T(8,128)} copy(s32[512,1]{0,1:T(1,128)} %bitcast.27) | data formatting | bytes 4096 | tf_op jit(solution)/shard_map/reshape | solution.py:572
  1.6 4.7 %prep.1 = (f32[2,32,384]{2,1,0:T(8,128)}, f32[32,768]{1,0:T(8,128)}, s32[512,128]{1,0:T(8,128)S(1)}, s32[8,128]{1,0:T(8,128)}, f32[32,2,32,384]{3,2,1,0:T(8,128)}) custom-call(s32[1]{0:T(128)} %bitcast.7.me_ref, s32[1,512]{1,0:T(1,128)} %bitcast.28, s32[512,1]{1,0:T(8,128)} %copy.7.pcol_ref, f32[768,768]{1,0:T(8,128)} %m_ref.1), custom_call_target="tpu_custom_call" | custom-call | tf_op jit(solution)/shard_map/prep/pallas_call | solution.py:95
  6.3 1.2 %slice.19 = s32[1,1]{1,0:T(1,128)} slice(s32[8,128]{1,0:T(8,128)} %get-tuple-element.145), slice={[0:1], [0:1]} | slice | bytes 8 | tf_op jit(solution)/shard_map/slice | solution.py:581
  8.1 0.0 copy-done.6
  8.1 0.0 copy-done.5
  8.1 90.5 %conditional.1 = (f32[768,768]{1,0:T(8,128)}) conditional(s32[]{:T(128)} %bitcast.10, (s32[512]{0:T(512)S(1)}, f32[768,768]{1,0:T(8,128)}, f32[64,512]{1,0:T(8,128)S(1)}) %tuple.76, (f32[64,512]{1,0:T(8,128)S(1)}, f32[2,32,384]{2,1,0:T(8,128)}, f32[32,2,32,384]{3,2,1,0:T(8,128)}, s32[1]{0:T(128)}, f32[768,768]{1,0:T(8,128)}, ...), branch_computations={%region_0.11_spmd, %region_11.12_spmd} | conditional | flops 13303746560 | bytes 176222848 | solution.py:581
  8.4 0.0 copy-start.7
  8.4 70.6 %exchange.1 = (f32[12,64,512]{2,1,0:T(8,128)}, f32[2,8,4,32,384]{4,3,2,1,0:T(8,128)}, f32[2,8,4,4,8,128]{5,4,3,2,1,0:T(8,128)}, f32[2,32,384]{2,1,0:T(8,128)}) custom-call(f32[64,512]{1,0:T(8,128)S(1)} %get-tuple-element.131.panel_ref, f32[2,32,384]{2,1,0:T(8,128)} %get-tuple-element.132.contrib_ref, f32[32,2,32,384]{3,2,1,0:T(8,128)} %get-tuple-element.133.top_ref), custom_call_target="tpu_custom_call" | custom-call | tf_op jit(solution)/shard_map/cond/branch_1_fun/exchange/pallas_call | solution.py:395
  79.0 0.0 copy-done.7
  79.0 19.7 %finish.1 = f32[768,768]{1,0:T(8,128)} custom-call(s32[1]{0:T(128)} %get-tuple-element.129.me_ref, f32[768,768]{1,0:T(8,128)} %get-tuple-element.130.m_ref, f32[768,512]{1,0:T(8,128)} %bitcast.26, f32[2,1024,384]{2,1,0:T(8,128)} %bitcast.25, f32[2,8,4,4,8,128]{5,4,3,2,1,0:T(8,128)} %get-tuple-element.136.low_ref, f32[2,32,384]{2,1,0:T(8,128)} %get-tuple-element.137.tops_ref, ...), custom_call_target="tpu_custom_call" | custom-call | tf_op jit(solution)/shard_map/cond/branch_1_fun/finish/pallas_call | solution.py:488
Async XLA Ops:
  0.0 8.1 %copy-start.6 = (s32[512]{0:T(512)S(1)}, s32[512]{0:T(512)}, u32[]{:S(2)}) copy-start(s32[512]{0:T(512)} %param.13) | copy-start | bytes 6148
  0.0 8.1 %copy-start.5 = (f32[64,512]{1,0:T(8,128)S(1)}, f32[64,512]{1,0:T(8,128)}, u32[]{:S(2)}) copy-start(f32[64,512]{1,0:T(8,128)} %param.12) | copy-start | bytes 393220
  8.4 70.6 %copy-start.7 = (f32[32,768]{1,0:T(8,128)S(1)}, f32[32,768]{1,0:T(8,128)}, u32[]{:S(2)}) copy-start(f32[32,768]{1,0:T(8,128)} %get-tuple-element.138.sel_ref) | copy-start | bytes 294916 | tf_op jit(solution)/shard_map/cond

commit v2 on v0

v2 whole, which is shorter than its diff:
```python
import functools

import jax
import jax.numpy as jnp
from jax import lax
from jax.experimental import pallas as pl
from jax.experimental.pallas import tpu as pltpu
from jax.sharding import PartitionSpec as P

NB = 512
NX, NY, NZ = 4, 8, 12
CHIPS = NX * NY
CAP = 32
MESH = pl.DeviceIdType.MESH
F32, BF16, I32 = jnp.float32, jnp.bfloat16, jnp.int32
HIGHEST = lax.Precision.HIGHEST


def mm(a, b, dims=((1,), (0,))):
    return lax.dot_general(a, b, (dims, ((), ())), preferred_element_type=F32)


def split3(v):
    hi = v.astype(BF16)
    rest = v - hi.astype(F32)
    mid = rest.astype(BF16)
    low = (rest - mid.astype(F32)).astype(BF16)
    return hi, mid, low


def select_rows(onehot, v, dims=((1,), (0,))):
    hi, mid, low = split3(v)
    return (mm(onehot, low, dims) + mm(onehot, mid, dims)) + mm(onehot, hi, dims)


def iota(shape, axis):
    return lax.broadcasted_iota(I32, shape, axis)


def chip_of(rows):
    return ((rows >> 9) * 171) >> 9


def count(mask, axis):
    return jnp.sum(mask.astype(F32), axis=axis, keepdims=True).astype(I32)


class Ring:
    def __init__(self, n, me, piece, device, send, recv):
        self.n, self.me, self.piece, self.device = n, me, piece, device
        self.send, self.recv = send, recv
        self.waited = set()

    def moves(self, s):
        last = s == self.n // 2 - 1
        return [(d, h) for h in (0, 1) for d in (0, 1) if not (last and d != h)]

    def copy(self, s, d, h, block):
        n = self.n
        ref = self.piece(lax.rem(block + 2 * n, n), h)
        peer = lax.rem(self.me + (1 if d == 0 else n - 1), n)
        return pltpu.make_async_remote_copy(
            src_ref=ref, dst_ref=ref,
            send_sem=self.send.at[d, s, h], recv_sem=self.recv.at[d, s, h],
            device_id=self.device(peer), device_id_type=MESH)

    def out(self, s, d, h):
        return self.copy(s, d, h, self.me - s if d == 0 else self.me + s)

    def arrive(self, s, d, h):
        block = self.me - 1 - s if d == 0 else self.me + 1 + s
        self.copy(s, d, h, block).wait_recv()
        self.waited.add((s, d, h))
        return lax.rem(block + 2 * self.n, self.n)

    def step(self, s, hook=None):
        for d, h in self.moves(s):
            if s > 0:
                block = self.arrive(s - 1, d, h)
                if hook is not None:
                    hook(block, h)
            self.out(s, d, h).start()

    def finish(self, hook=None):
        for s in range(self.n // 2):
            for d, h in self.moves(s):
                if (s, d, h) not in self.waited:
                    block = self.arrive(s, d, h)
                    if hook is not None:
                        hook(block, h)

    def drain(self):
        for s in range(self.n // 2):
            for d, h in self.moves(s):
                self.out(s, d, h).wait_send()


def hdot(a, b):
    return jnp.dot(a, b, precision=HIGHEST, preferred_element_type=F32)


def step_kernel(prow_ref, panel_ref, matrix_ref,
                out_ref, most_ref,
                mat, pall, slots_all, low_all, tops, staged, relay,
                from_pair, contrib, own, low_in, keys, parts,
                lower, inverse, perm, p_hi, p_lo, upper, prod,
                z_send, z_recv, r_send, r_recv, q_send, q_recv,
                one_send, one_recv, lone_send, lone_recv,
                zl_send, zl_recv, sc_send, sc_recv, local,
                pair_send, pair_recv, slot_send, slot_recv,
                lpair_send, lpair_recv, top_send, top_recv, tp_send, tp_recv,
                rl_send, rl_recv, rs_send):
    pr = lax.axis_index("prow")
    z = lax.axis_index("pcol")
    core = lax.rem(pr, 2)
    chip = pr // 2
    x = lax.rem(chip, NX)
    y = chip // NX
    rows, cols = mat.shape
    half = cols // 2

    def dev(x=x, y=y, c=core, z=z):
        return ((y * NX + x) * 2 + c, z)

    def remote(src, dst, ss, rs, device):
        return pltpu.make_async_remote_copy(
            src_ref=src, dst_ref=dst, send_sem=ss, recv_sem=rs,
            device_id=device, device_id_type=MESH)

    partner = dev(c=1 - core)
    is_root = pr == 0
    fetch = pltpu.make_async_copy(matrix_ref, mat, local.at[5])
    fetch.start()
    own_panel = pltpu.make_async_copy(panel_ref, pall.at[z], local.at[0])
    own_panel.start()
    barrier = pltpu.get_barrier_semaphore()

    def hello(device):
        pl.semaphore_signal(barrier, inc=1, device_id=device, device_id_type=MESH)

    for d in range(1, NZ):
        hello(dev(z=lax.rem(z + d, NZ)))
    for d in range(1, NX):
        hello(dev(x=lax.rem(x + d, NX)))
    for d in range(1, NY):
        hello(dev(y=lax.rem(y + d, NY)))
    hello(partner)
    near = NZ + NX + NY - 2

    @pl.when(is_root)
    def _():
        @pl.loop(1, 2 * CHIPS)
        def _(q):
            hello((q, z))

    @pl.when(jnp.logical_not(is_root))
    def _():
        hello((0, z))

    p_r = prow_ref[...]
    c_r = chip_of(p_r)
    here = c_r == chip
    before = (iota((NB, NB), 0) < iota((NB, NB), 1)).astype(BF16)
    rank = mm(jnp.broadcast_to(here.astype(BF16), (16, NB)), before)[:1].astype(I32)
    mine_at = here & (rank == iota((CAP, NB), 0))
    row = jnp.sum(jnp.where(mine_at, (p_r + 1).astype(F32), 0.0), axis=1, keepdims=True).astype(I32) - 1
    pick = (row - pr * rows) == iota((CAP, rows), 1)
    sel = (pick & (row >= NB)).astype(BF16)
    fetch.wait()
    got = select_rows(pick.astype(BF16), mat[...])
    contrib[0] = got[:, :half]
    contrib[1] = got[:, half:]
    own_panel.wait()

    @pl.when(is_root)
    def _():
        pl.semaphore_wait(barrier, near + 2 * CHIPS - 1)

    @pl.when(jnp.logical_not(is_root))
    def _():
        pl.semaphore_wait(barrier, near + 1)

    def line(mine):
        other = 1 - mine
        n1, n2 = (NX, NY) if mine == 0 else (NY, NX)
        a1, a2 = (x, y) if mine == 0 else (y, x)
        peer1 = (lambda i: dev(x=i)) if mine == 0 else (lambda i: dev(y=i))
        peer2 = (lambda i: dev(y=i)) if mine == 0 else (lambda i: dev(x=i))
        slots = slots_all.at[mine]
        lows = low_all.at[mine]
        low_root = is_root & (z < NB // 64)
        has_low = (z < NB // 64) & (lax.rem(z, 2) == mine)
        top_here = is_root if mine == 0 else (pr < 0)

        def part(ref):
            if mine == 0:
                return lambda b, h: ref.at[b, pl.ds(2 * h, 2)]
            return lambda b, h: ref.at[pl.ds(4 * h, 4), b]

        zr = Ring(NZ, z, lambda b, h: pall.at[b, pl.ds(32 * h, 32)],
                  lambda i: dev(z=i), z_send, z_recv)
        ring = Ring(n2, a2, part(slots), peer2, r_send, r_recv)
        lring = Ring(n2, a2, part(lows), peer2, q_send, q_recv)
        last = n2 // 2 - 1
        pair = lambda: remote(contrib.at[other], from_pair, pair_send, pair_recv, partner)
        keep = lambda: pltpu.make_async_copy(own, slots.at[y, x], local.at[2])
        keep_low = lambda: pltpu.make_async_copy(low_in, lows.at[y, x, z // 2], local.at[3])

        def spread(d):
            return remote(own, slots.at[y, x], one_send.at[d], one_recv.at[d],
                          peer1(lax.rem(a1 + d, n1)))

        def lspread(d):
            return remote(lows.at[y, x], lows.at[y, x], lone_send.at[d], lone_recv.at[d],
                          peer1(lax.rem(a1 + d, n1)))

        def zspread(d):
            return remote(low_in, lows.at[y, x, z // 2], zl_send.at[d], zl_recv.at[z // 2],
                          dev(z=lax.rem(z + d, NZ)))

        def spread_wait(ref, ss, rs):
            for d in range(1, n1):
                src = lax.rem(a1 + n1 - d, n1)
                dst = ref.at[y, src] if mine == 0 else ref.at[src, x]
                remote(dst, dst, ss.at[d], rs.at[d], peer1(src)).wait_recv()

        def to_pair(block, h):
            ref = part(slots)(block, h)
            remote(ref, ref, slot_send, slot_recv, partner).start()

        def seg0():
            zr.step(0)

            @pl.when(low_root)
            def _():
                @pl.loop(0, CHIPS)
                def _(q):
                    src = panel_ref.at[pl.ds(pl.multiple_of(q // NX * 8, 8), 8),
                                       pl.ds(pl.multiple_of(lax.rem(q, NX) * 128, 128), 128)]

                    @pl.when((q > 0) | (lax.rem(z, 2) == 1))
                    def _():
                        remote(src, low_in, sc_send.at[q], sc_recv,
                               (q * 2 + lax.rem(z, 2), z)).start()

            pair().start()

            @pl.when(is_root & has_low)
            def _():
                tile = pltpu.make_async_copy(panel_ref.at[pl.ds(0, 8), pl.ds(0, 128)], low_in, local.at[1])
                tile.start()
                tile.wait()

            pair().wait_recv()
            own[...] = contrib[mine] + from_pair[...]
            keep().start()
            for d in range(1, n1):
                spread(d).start()

        def seg1():
            @pl.when(has_low)
            def _():
                @pl.when(jnp.logical_not(top_here))
                def _():
                    remote(low_in, low_in, sc_send.at[0], sc_recv, partner).wait_recv()
                keep_low().start()
                for d in range(1, NZ):
                    zspread(d).start()
            zr.step(1)

        def seg2():
            keep().wait()
            spread_wait(slots, one_send, one_recv)
            ring.step(0)
            for h in (0, 1):
                to_pair(a2, h)
            zr.step(2)

        def seg3():
            for i in range(4):
                @pl.when(z != 2 * i + mine)
                def _():
                    ref = lows.at[y, x, i]
                    remote(ref, ref, zl_send.at[1], zl_recv.at[i], partner).wait_recv()

            @pl.when(has_low)
            def _():
                keep_low().wait()
            for d in range(1, n1):
                lspread(d).start()
            ring.step(1, to_pair)
            zr.step(3)

        def seg4():
            spread_wait(lows, lone_send, lone_recv)
            lring.step(0)
            if last >= 2:
                ring.step(2, to_pair)
            zr.step(4)
            lring.step(1)

        def seg5():
            if last >= 3:
                ring.step(3, to_pair)
                lring.step(2)
            zr.step(5)
            if last >= 3:
                lring.step(3)
            ring.finish(to_pair)
            if mine == 0:
                @pl.when(is_root)
                def _():
                    remote(staged.at[0, 0, 1], tops.at[1], top_send.at[0, 1], top_recv, partner).start()
                    for c in (0, 1):
                        for q in (1, 3):
                            via(q, c).start()

                    @pl.loop(1, CHIPS)
                    def _(q):
                        xx, yy = lax.rem(q, NX), q // NX

                        @pl.when((lax.rem(xx, 2) == 0) | (yy == 0))
                        def _():
                            for c in (0, 1):
                                remote(staged.at[yy, xx, c], tops.at[c], top_send.at[q, c], top_recv,
                                       (q * 2 + c, z)).start()
            zr.finish()
            ref = slots_all.at[other]
            remote(ref, ref, slot_send, slot_recv, partner).wait_recv()

        def via(q, c):
            return remote(staged.at[pl.ds(1, NY - 1), q, c], relay,
                          rl_send.at[q // 2, c], rl_recv, (q * 2 + c, z))

        def seg6():
            lring.finish()
            remote(lows, lows, lpair_send, lpair_recv, partner).start()
            ref = low_all.at[other]
            remote(ref, ref, lpair_send, lpair_recv, partner).wait_recv()

        relays = (y == 0) & (lax.rem(x, 2) == 1)

        def onward(i):
            return remote(relay.at[i], tops.at[mine], rs_send.at[i], top_recv, dev(y=i + 1))

        def seg7():
            @pl.when(relays)
            def _():
                remote(relay, relay, rl_send.at[0, 0], rl_recv, partner).wait_recv()
                for i in range(NY - 1):
                    onward(i).start()

        def tpair():
            return remote(tops.at[mine], tops.at[mine], tp_send, tp_recv, partner)

        def seg8():
            @pl.when(jnp.logical_not(top_here))
            def _():
                remote(tops.at[mine], tops.at[mine], top_send.at[0, 0], top_recv, partner).wait_recv()
            if mine == 0:
                @pl.when(is_root)
                def _():
                    first = pltpu.make_async_copy(staged.at[0, 0, 0], tops.at[0], local.at[4])
                    first.start()
                    first.wait()
            tpair().start()
            ref = tops.at[other]
            remote(ref, ref, tp_send, tp_recv, partner).wait_recv()

        def seg9():
            pair().wait_send()
            for d in range(1, n1):
                spread(d).wait_send()
                lspread(d).wait_send()
            remote(lows, lows, lpair_send, lpair_recv, partner).wait_send()
            tpair().wait_send()
            ring.drain()
            lring.drain()
            zr.drain()
            remote(slots, slots, slot_send, slot_recv, partner).wait_send()

            @pl.when(has_low)
            def _():
                for d in range(1, NZ):
                    zspread(d).wait_send()

            @pl.when(low_root & (mine == 0))
            def _():
                @pl.loop(0, CHIPS)
                def _(q):
                    @pl.when((q > 0) | (lax.rem(z, 2) == 1))
                    def _():
                        remote(low_in, low_in, sc_send.at[q], sc_recv, partner).wait_send()

            @pl.when(relays)
            def _():
                for i in range(NY - 1):
                    onward(i).wait_send()

            if mine == 0:
                @pl.when(is_root)
                def _():
                    remote(staged.at[0, 0, 1], tops.at[1], top_send.at[0, 1], top_recv, partner).wait_send()
                    for c in (0, 1):
                        for q in (1, 3):
                            via(q, c).wait_send()

                    @pl.loop(1, CHIPS)
                    def _(q):
                        xx, yy = lax.rem(q, NX), q // NX

                        @pl.when((lax.rem(xx, 2) == 0) | (yy == 0))
                        def _():
                            for c in (0, 1):
                                remote(staged.at[yy, xx, c], tops.at[c], top_send.at[q, c], top_recv,
                                       partner).wait_send()

        return [seg0, seg1, seg2, seg3, seg4, seg5, seg6, seg7, seg8, seg9]

    segments = [line(0), line(1)]

    def run(k):
        for mine in (0, 1):
            pl.when(core == mine)(segments[mine][k])

    def column(v):
        wide = jnp.broadcast_to(v.astype(F32), (128, NB)).T.astype(I32)
        return jnp.concatenate([wide] * (NB // 128), axis=1)

    def top_index():
        p_c = column(p_r)
        c_c = chip_of(p_c)
        i0, i1 = iota((NB, NB), 0), iota((NB, NB), 1)
        d_r = c_r * CAP + count((c_c == c_r) & (i0 < i1), 0)
        t_r = iota((1, NB), 1)
        left_rank = t_r - count(p_c < t_r, 0)
        chosen = count(p_c == t_r, 0) > 0
        vac_rank = count((p_c >= NB) & (p_c < p_r), 0)
        keys[0:1] = d_r
        keys[1:2] = jnp.where(chosen, -2, left_rank)
        keys[2:3] = jnp.where(p_r >= NB, vac_rank + 1, 0)
        for i, piece in enumerate(split3(mat[:NB])):
            parts[i] = piece

    def top_piece(g):
        n = 8 * CAP
        e = keys[0:1] == g * n + iota((n, NB), 0)
        key = jnp.sum(jnp.where(e, keys[2:3].astype(F32), 0.0), axis=1, keepdims=True).astype(I32) - 1
        onehot = (key == keys[1:2]).astype(BF16)
        res = (mm(onehot, parts[2]) + mm(onehot, parts[1])) + mm(onehot, parts[0])
        for c in (0, 1):
            staged[pl.ds(2 * g, 2), :, c] = res[:, c * half:c * half + half].reshape(2, NX, CAP, half)

    def on_root(*work):
        @pl.when(is_root)
        def _():
            for w in work:
                w()

    run(0)
    on_root(top_index, lambda: top_piece(0))
    run(1)
    run(2)
    on_root(lambda: top_piece(1), lambda: top_piece(2))
    p_c = column(p_r)
    c_c = chip_of(p_c)
    slot_c = jnp.sum(((c_c == c_r) & (iota((NB, NB), 1) < iota((NB, NB), 0))).astype(F32),
                     axis=1, keepdims=True)
    most_ref[0] = jnp.max(slot_c)
    dest = c_c[:, :128] * CAP + jnp.broadcast_to(slot_c.astype(I32), (NB, 128))
    for k in range(CHIPS * CAP // 128):
        perm[:, 128 * k:128 * k + 128] = (dest == iota((NB, 128), 1) + 128 * k).astype(BF16)
    run(3)
    on_root(lambda: top_piece(3))
    run(4)
    run(5)

    @pl.loop(0, 2)
    def _(n):
        upper[n] = select_rows(perm[...], slots_all[n].reshape(CHIPS * CAP, half))

    full = pall[...].reshape(rows, NB)
    hi = full.astype(BF16)
    p_hi[...] = hi
    p_lo[...] = (full - hi.astype(F32)).astype(BF16)
    run(6)
    for i in range(NB // 64):
        for yy in range(NY):
            for xx in range(NX):
                if 128 * xx < 64 * i + 64:
                    lower[64 * i + 8 * yy:64 * i + 8 * yy + 8, 128 * xx:128 * xx + 128] = (
                        low_all[i % 2, yy, xx, i // 2])
    i0, i1 = iota((128, 128), 0), iota((128, 128), 1)
    eye = (i0 == i1).astype(F32)
    diag = [lower[128 * k:128 * k + 128, 128 * k:128 * k + 128] for k in range(4)]
    size = 1
    invs = [eye] * 4
    while size < 128:
        mask = ((i0 // (2 * size)) == (i1 // (2 * size))) & (
            (i0 // size) % 2 == 1) & ((i1 // size) % 2 == 0)
        offs = [jnp.where(mask, d, 0.0) for d in diag]
        if size == 1:
            invs = [eye - o for o in offs]
        else:
            mids = [hdot(o, v) for o, v in zip(offs, invs)]
            invs = [v - hdot(v, t) for v, t in zip(invs, mids)]
        size *= 2
    for k in range(4):
        inverse[k] = invs[k]
    run(7)

    @pl.loop(0, 2)
    def _(n):
        for i in range(4):
            rhs = upper[n, 128 * i:128 * i + 128]
            if i:
                rhs = rhs - hdot(lower[128 * i:128 * i + 128, :128 * i], upper[n, :128 * i])
            upper[n, 128 * i:128 * i + 128] = hdot(inverse[i], rhs)
        u = upper[n]
        u_hi = u.astype(BF16)
        u_lo = (u - u_hi.astype(F32)).astype(BF16)
        prod[n] = (mm(p_lo[...], u_hi) + mm(p_hi[...], u_lo)) + mm(p_hi[...], u_hi)

    run(8)
    replaced = mm(sel, jnp.ones((CAP, 128), BF16), ((0,), (0,)))[:, :1] > 0.5
    for n in (0, 1):
        at = slice(n * half, n * half + half)
        incoming = select_rows(sel, tops[n], ((0,), (0,)))
        prod[n] = jnp.where(replaced, incoming, mat[:, at]) - prod[n]

        @pl.when(is_root)
        def _():
            prod[n, :NB] = upper[n]
        pltpu.make_async_copy(prod.at[n], out_ref.at[:, pl.ds(n * half, half)], local.at[6 + n]).start()
    run(9)
    for n in (0, 1):
        pltpu.make_async_copy(prod.at[n], out_ref.at[:, pl.ds(n * half, half)], local.at[6 + n]).wait()


def step(p_row, panel, matrix):
    rows, cols = matrix.shape
    half = cols // 2
    dma = pltpu.SemaphoreType.DMA
    vm = pl.BlockSpec(memory_space=pltpu.VMEM)
    anyspec = pl.BlockSpec(memory_space=pl.ANY)
    v = pltpu.VMEM
    return pl.pallas_call(
        step_kernel,
        out_shape=(
            jax.ShapeDtypeStruct((rows, cols), F32),
            jax.ShapeDtypeStruct((1,), F32),
        ),
        in_specs=[vm, vm, anyspec],
        out_specs=(anyspec, pl.BlockSpec(memory_space=pltpu.SMEM)),
        scratch_shapes=[
            v((rows, cols), F32), v((NZ,) + panel.shape, F32),
            v((2, NY, NX, CAP, half), F32), v((2, NY, NX, 4, 8, 128), F32),
            v((2, CAP, half), F32), v((NY, NX, 2, CAP, half), F32), v((NY - 1, CAP, half), F32),
            v((CAP, half), F32), v((2, CAP, half), F32), v((CAP, half), F32), v((8, 128), F32),
            v((8, NB), I32), v((3, NB, cols), BF16),
            v((NB, NB), F32), v((4, 128, 128), F32), v((NB, CHIPS * CAP), BF16),
            v((rows, NB), BF16), v((rows, NB), BF16), v((2, NB, half), F32), v((2, rows, half), F32),
            dma((2, NZ // 2, 2)), dma((2, NZ // 2, 2)),
            dma((2, NY // 2, 2)), dma((2, NY // 2, 2)),
            dma((2, NY // 2, 2)), dma((2, NY // 2, 2)),
            dma((NY,)), dma((NY,)), dma((NY,)), dma((NY,)),
            dma((NZ,)), dma((4,)), dma((CHIPS,)), dma, dma((8,)),
            dma, dma, dma, dma, dma, dma, dma((CHIPS, 2)), dma, dma, dma,
            dma((2, 2)), dma, dma((NY - 1,)),
        ],
        compiler_params=pltpu.CompilerParams(collective_id=0, has_side_effects=True),
        name="step",
    )(p_row, panel, matrix)


def ring_sum(value, axis):
    n = lax.axis_size(axis)
    pairs = [(i, (i + 1) % n) for i in range(n)]

    def body(_, carry):
        total, moving = carry
        moving = lax.ppermute(moving, axis, pairs)
        return total + moving, moving

    return lax.fori_loop(0, n - 1, body, (value, value))[0]


def dense(matrix, panel, pivot_rows):
    own_rows = matrix.shape[0]
    row = lax.axis_index("prow")
    col = lax.axis_index("pcol")
    row_base = row * own_rows
    slab = jnp.zeros((lax.axis_size("pcol"),) + panel.shape, F32)
    panels = ring_sum(lax.dynamic_update_slice(slab, panel[None], (col, 0, 0)), "pcol")
    panels = panels.reshape(own_rows, NB)
    local_rows = pivot_rows - row_base
    owned = (local_rows >= 0) & (local_rows < own_rows)
    picked = (local_rows[:, None] == jnp.arange(own_rows, dtype=I32)[None, :]).astype(F32)
    picked = jnp.dot(picked, matrix, precision=HIGHEST, preferred_element_type=F32)
    first = jnp.where(row == 0, 1.0, 0.0)
    pack = jnp.concatenate([picked, matrix[:NB] * first], axis=1)
    pack = jnp.concatenate([pack, panels[:NB] * first], axis=1)
    pack = ring_sum(pack, "prow")
    own_cols = matrix.shape[1]
    new_top, top_rows, lower = pack[:, :own_cols], pack[:, own_cols:2 * own_cols], pack[:, 2 * own_cols:]

    def solve_row(j, upper):
        coef = lax.dynamic_slice(lower, (j, 0), (1, NB))
        coef = jnp.where(jnp.arange(NB)[None, :] < j, coef, 0.0)
        done = jnp.dot(coef, upper, precision=HIGHEST, preferred_element_type=F32)
        mine = lax.dynamic_slice(upper, (j, 0), (1, own_cols)) - done
        return lax.dynamic_update_slice(upper, mine, (j, 0))

    upper = lax.fori_loop(0, NB, solve_row, new_top)
    vacated = pivot_rows >= NB
    top_index = jnp.arange(NB, dtype=I32)
    chosen = jnp.any(pivot_rows[None, :] == top_index[:, None], axis=1)
    left_rank = top_index - jnp.sum((pivot_rows[None, :] < top_index[:, None]).astype(I32), axis=1)
    vac_rank = jnp.sum((vacated[None, :] & (pivot_rows[None, :] < pivot_rows[:, None])).astype(I32), axis=1)
    pairing = (vacated[:, None] & jnp.logical_not(chosen)[None, :]
               & (left_rank[None, :] == vac_rank[:, None])).astype(F32)
    incoming = jnp.dot(pairing, top_rows, precision=HIGHEST, preferred_element_type=F32)
    global_rows = row_base + jnp.arange(own_rows, dtype=I32)
    place = (global_rows[:, None] == pivot_rows[None, :]) & vacated[None, :]
    moved = jnp.dot(place.astype(F32), incoming, precision=HIGHEST, preferred_element_type=F32)
    swapped = jnp.where(jnp.any(place, axis=1)[:, None], moved, matrix)
    updated = swapped - jnp.dot(panels, upper, precision=HIGHEST, preferred_element_type=F32)
    top_fill = jnp.pad(upper, ((0, own_rows - NB), (0, 0)))
    return jnp.where((global_rows < NB)[:, None], top_fill, updated)


def shards(matrix, panel, pivot_rows):
    out, most = step(pivot_rows.reshape(1, NB), panel, matrix)
    return lax.cond(most[0] < CAP, lambda: out, lambda: dense(matrix, panel, pivot_rows))


def solution(mesh):
    return jax.shard_map(
        shards,
        mesh=mesh,
        in_specs=(P("prow", "pcol"), P(("prow", "pcol"), None), P()),
        out_specs=P("prow", "pcol"),
        check_vma=False,
    )
```

time: 378 us -> 74.6 us (0.20); the launches traced: 371 us -> 74.4 us
  waiting for transfers between devices: 262 us -> 0 us
  Pallas kernels: 0 us -> 70.5 us
  other arithmetic: 56.4 us -> 0 us
  local copies, waits for them, and re-layouts: 25.9 us -> 3.23 us
  matrix products: 14 us -> 0 us
  between operations: 13.3 us -> 0.65 us
    psum x1 -> x0, waiting for transfers between devices: 221 us -> none  [from_root(): return lax.psum(kept, axis)]
    pallas_call x0 -> x1, Pallas kernels: none -> 70.5 us  [step(): pl.pallas_call(step_kernel, out_shape=(jax.ShapeDtypeStruct((rows, cols),...]
    another operation x7 -> x0, other arithmetic: 43.8 us -> none  [the longest x5 43.4 us: shards(): lax.linalg.triangular_solve(lower_block, new_top, left_side=True, lower=T...]
    all_gather x2 -> x0, waiting for transfers between devices: 40.2 us -> none  [the longest x1 40.2 us: shards(): lower_block = lax.all_gather(lead_panel, 'pcol', axis=0, tiled=True)[:NB]]
    another operation x15 -> x0, local copies, waits for them, and re-layouts: 11 us -> none
    dot_general x1 -> x0, matrix products: 7.84 us -> none  [shards(): jnp.dot(lax.all_gather(panel, 'pcol', axis=0, tiled=True), upper_block, p...]
    scatter x1 -> x0, other arithmetic: 7.49 us -> none  [shards(): swapped = matrix.at[target].set(incoming, mode='drop')]
    another operation x7 -> x0, matrix products: 6.15 us -> none  [shards(): lax.linalg.triangular_solve(lower_block, new_top, left_side=True, lower=T...]
  transfers between devices with their start and end apart: 3 -> 0, of which waited for: 2 -> 0; matrix products, arithmetic and copies ran while one was open for 20% -> 0% of each run, Pallas kernels for 0% -> 0%
where the time goes in v2:
time: 74.6 us; the launch traced here: 74.4 us
  Pallas kernels  70.5 us (95%)
  local copies, waits for them, and re-layouts  3.23 us (4%)
    pallas_call x1, Pallas kernels, step(): pl.pallas_call(step_kernel, out_shape=(jax.ShapeDtypeStruct((rows, cols),...  70.5 us
    unnamed x5, local copies, waits for them, and re-layouts  3.23 us

profile of v2, /device:TPU:1, one launch (start us, length us, event | category | flops | bytes accessed | tf_op | source)
XLA Modules:
  0.0 74.4 jit_solution(17102123444553182850)
XLA Ops:
  0.0 0.0 copy-start.6
  0.0 0.0 copy-start.5
  0.0 70.5 %step.1 = (f32[768,768]{1,0:T(8,128)}, f32[1]{0:T(128)}) custom-call(s32[1,512]{1,0:T(1,128)} %bitcast.21, f32[64,512]{1,0:T(8,128)} %panel_ref.1, f32[768,768]{1,0:T(8,128)} %matrix_ref.1), custom_call_target="tpu_custom_call" | custom-call | tf_op jit(solution)/shard_map/step/pallas_call | solution.py:547
  71.1 0.0 copy-done.6
  71.2 0.0 copy-done.5
  71.2 3.2 %copy.35 = f32[768,768]{1,0:T(8,128)} copy(f32[768,768]{1,0:T(8,128)} %get-tuple-element.120) | data formatting | bytes 4718592
  (1 shorter events, 0.0 us)
Async XLA Ops:
  0.0 71.1 %copy-start.6 = (s32[512]{0:T(512)S(1)}, s32[512]{0:T(512)}, u32[]{:S(2)}) copy-start(s32[512]{0:T(512)} %param.13) | copy-start | bytes 6148
  0.0 71.2 %copy-start.5 = (f32[64,512]{1,0:T(8,128)S(1)}, f32[64,512]{1,0:T(8,128)}, u32[]{:S(2)}) copy-start(f32[64,512]{1,0:T(8,128)} %panel_ref.1) | copy-start | bytes 393220

commit v3 on v2

--- a/solution.py
+++ b/solution.py
@@ -99,11 +99,24 @@
     return jnp.dot(a, b, precision=HIGHEST, preferred_element_type=F32)
 
 
+def halves_inverse(diag, size_to):
+    i0, i1 = iota(diag.shape, 0), iota(diag.shape, 1)
+    inv = (i0 == i1).astype(F32)
+    size = 1
+    while size < size_to:
+        mask = ((i0 // (2 * size)) == (i1 // (2 * size))) & (
+            (i0 // size) % 2 == 1) & ((i1 // size) % 2 == 0)
+        off = jnp.where(mask, diag, 0.0)
+        inv = inv - (off if size == 1 else hdot(inv, hdot(off, inv)))
+        size *= 2
+    return inv
+
+
 def step_kernel(prow_ref, panel_ref, matrix_ref,
-                out_ref, most_ref,
+                u_ref, p_ref, tops_ref, sel_ref, most_ref,
                 mat, pall, slots_all, low_all, tops, staged, relay,
                 from_pair, contrib, own, low_in, keys, parts,
-                lower, inverse, perm, p_hi, p_lo, upper, prod,
+                low_src, lower, inverse, perm, upper, sel,
                 z_send, z_recv, r_send, r_recv, q_send, q_recv,
                 one_send, one_recv, lone_send, lone_recv,
                 zl_send, zl_recv, sc_send, sc_recv, local,
@@ -165,12 +178,27 @@
     mine_at = here & (rank == iota((CAP, NB), 0))
     row = jnp.sum(jnp.where(mine_at, (p_r + 1).astype(F32), 0.0), axis=1, keepdims=True).astype(I32) - 1
     pick = (row - pr * rows) == iota((CAP, rows), 1)
-    sel = (pick & (row >= NB)).astype(BF16)
+    sel[...] = (pick & (row >= NB)).astype(F32)
+    keep_sel = pltpu.make_async_copy(sel, sel_ref, local.at[6])
     fetch.wait()
     got = select_rows(pick.astype(BF16), mat[...])
     contrib[0] = got[:, :half]
     contrib[1] = got[:, half:]
     own_panel.wait()
+
+    @pl.when(is_root & (z < NB // 64))
+    def _():
+        at = iota((64, NB), 1) == iota((64, NB), 0) + 64 * z
+        pan = panel_ref[...]
+        hi, mid, low = split3(pan)
+        onto = at.astype(BF16)
+        to = ((1,), (1,))
+        diag = (mm(low, onto, to) + mm(mid, onto, to)) + mm(hi, onto, to)
+        inv = halves_inverse(diag, 64)
+        hi, mid, low = split3(inv)
+        back = (mm(low, onto) + mm(mid, onto)) + mm(hi, onto)
+        col = iota((64, NB), 1)
+        low_src[...] = jnp.where((col >= 64 * z) & (col < 64 * z + 64), back, pan)
 
     @pl.when(is_root)
     def _():
@@ -235,7 +263,7 @@
             def _():
                 @pl.loop(0, CHIPS)
                 def _(q):
-                    src = panel_ref.at[pl.ds(pl.multiple_of(q // NX * 8, 8), 8),
+                    src = low_src.at[pl.ds(pl.multiple_of(q // NX * 8, 8), 8),
                                        pl.ds(pl.multiple_of(lax.rem(q, NX) * 128, 128), 128)]
 
                     @pl.when((q > 0) | (lax.rem(z, 2) == 1))
@@ -247,7 +275,7 @@
 
             @pl.when(is_root & has_low)
             def _():
-                tile = pltpu.make_async_copy(panel_ref.at[pl.ds(0, 8), pl.ds(0, 128)], low_in, local.at[1])
+                tile = pltpu.make_async_copy(low_src.at[pl.ds(0, 8), pl.ds(0, 128)], low_in, local.at[1])
                 tile.start()
                 tile.wait()
 
@@ -269,42 +297,41 @@
             zr.step(1)
 
         def seg2():
+            zr.step(2)
+            for i in range(4):
+                @pl.when(z != 2 * i + mine)
+                def _():
+                    ref = lows.at[y, x, i]
+                    remote(ref, ref, zl_send.at[1], zl_recv.at[i], partner).wait_recv()
+
+            @pl.when(has_low)
+            def _():
+                keep_low().wait()
+            for d in range(1, n1):
+                lspread(d).start()
             keep().wait()
             spread_wait(slots, one_send, one_recv)
             ring.step(0)
             for h in (0, 1):
                 to_pair(a2, h)
-            zr.step(2)
 
         def seg3():
-            for i in range(4):
-                @pl.when(z != 2 * i + mine)
-                def _():
-                    ref = lows.at[y, x, i]
-                    remote(ref, ref, zl_send.at[1], zl_recv.at[i], partner).wait_recv()
-
-            @pl.when(has_low)
-            def _():
-                keep_low().wait()
-            for d in range(1, n1):
-                lspread(d).start()
-            ring.step(1, to_pair)
             zr.step(3)
-
-        def seg4():
             spread_wait(lows, lone_send, lone_recv)
             lring.step(0)
+            ring.step(1, to_pair)
+
+        def seg4():
+            zr.step(4)
+            lring.step(1)
             if last >= 2:
                 ring.step(2, to_pair)
-            zr.step(4)
-            lring.step(1)
 
         def seg5():
-            if last >= 3:
-                ring.step(3, to_pair)
-                lring.step(2)
             zr.step(5)
             if last >= 3:
+                lring.step(2)
+                ring.step(3, to_pair)
                 lring.step(3)
             ring.finish(to_pair)
             if mine == 0:
@@ -325,6 +352,8 @@
                                 remote(staged.at[yy, xx, c], tops.at[c], top_send.at[q, c], top_recv,
                                        (q * 2 + c, z)).start()
             zr.finish()
+            lring.finish()
+            remote(lows, lows, lpair_send, lpair_recv, partner).start()
             ref = slots_all.at[other]
             remote(ref, ref, slot_send, slot_recv, partner).wait_recv()
 
@@ -333,8 +362,6 @@
                           rl_send.at[q // 2, c], rl_recv, (q * 2 + c, z))
 
         def seg6():
-            lring.finish()
-            remote(lows, lows, lpair_send, lpair_recv, partner).start()
             ref = low_all.at[other]
             remote(ref, ref, lpair_send, lpair_recv, partner).wait_recv()
 
@@ -458,6 +485,7 @@
                 w()
 
     run(0)
+    keep_sel.start()
     on_root(top_index, lambda: top_piece(0))
     run(1)
     run(2)
@@ -474,15 +502,11 @@
     on_root(lambda: top_piece(3))
     run(4)
     run(5)
-
-    @pl.loop(0, 2)
-    def _(n):
-        upper[n] = select_rows(perm[...], slots_all[n].reshape(CHIPS * CAP, half))
-
-    full = pall[...].reshape(rows, NB)
-    hi = full.astype(BF16)
-    p_hi[...] = hi
-    p_lo[...] = (full - hi.astype(F32)).astype(BF16)
+    keep_panel = pltpu.make_async_copy(pall, p_ref, local.at[7])
+    keep_panel.start()
+    for n in (0, 1):
+        upper[:, n * half:n * half + half] = select_rows(
+            perm[...], slots_all[n].reshape(CHIPS * CAP, half))
     run(6)
     for i in range(NB // 64):
         for yy in range(NY):
@@ -491,50 +515,32 @@
                     lower[64 * i + 8 * yy:64 * i + 8 * yy + 8, 128 * xx:128 * xx + 128] = (
                         low_all[i % 2, yy, xx, i // 2])
     i0, i1 = iota((128, 128), 0), iota((128, 128), 1)
-    eye = (i0 == i1).astype(F32)
-    diag = [lower[128 * k:128 * k + 128, 128 * k:128 * k + 128] for k in range(4)]
-    size = 1
-    invs = [eye] * 4
-    while size < 128:
-        mask = ((i0 // (2 * size)) == (i1 // (2 * size))) & (
-            (i0 // size) % 2 == 1) & ((i1 // size) % 2 == 0)
-        offs = [jnp.where(mask, d, 0.0) for d in diag]
-        if size == 1:
-            invs = [eye - o for o in offs]
-        else:
-            mids = [hdot(o, v) for o, v in zip(offs, invs)]
-            invs = [v - hdot(v, t) for v, t in zip(invs, mids)]
-        size *= 2
     for k in range(4):
-        inverse[k] = invs[k]
+        block = lower[128 * k:128 * k + 128, 128 * k:128 * k + 128]
+        two = jnp.where((i0 // 64) == (i1 // 64), block, 0.0)
+        off = jnp.where(i0 // 64 > i1 // 64, block, 0.0)
+        inverse[k] = two - hdot(two, hdot(off, two))
     run(7)
 
-    @pl.loop(0, 2)
-    def _(n):
-        for i in range(4):
-            rhs = upper[n, 128 * i:128 * i + 128]
-            if i:
-                rhs = rhs - hdot(lower[128 * i:128 * i + 128, :128 * i], upper[n, :128 * i])
-            upper[n, 128 * i:128 * i + 128] = hdot(inverse[i], rhs)
-        u = upper[n]
-        u_hi = u.astype(BF16)
-        u_lo = (u - u_hi.astype(F32)).astype(BF16)
-        prod[n] = (mm(p_lo[...], u_hi) + mm(p_hi[...], u_lo)) + mm(p_hi[...], u_hi)
-
+    def keep_upper(i):
+        return pltpu.make_async_copy(upper.at[pl.ds(128 * i, 128)], u_ref.at[pl.ds(128 * i, 128)],
+                                     local.at[8 + i])
+
+    for i in range(4):
+        rhs = upper[128 * i:128 * i + 128]
+        if i:
+            rhs = rhs - hdot(lower[128 * i:128 * i + 128, :128 * i], upper[:128 * i])
+        upper[128 * i:128 * i + 128] = hdot(inverse[i], rhs)
+        keep_upper(i).start()
     run(8)
-    replaced = mm(sel, jnp.ones((CAP, 128), BF16), ((0,), (0,)))[:, :1] > 0.5
-    for n in (0, 1):
-        at = slice(n * half, n * half + half)
-        incoming = select_rows(sel, tops[n], ((0,), (0,)))
-        prod[n] = jnp.where(replaced, incoming, mat[:, at]) - prod[n]
-
-        @pl.when(is_root)
-        def _():
-            prod[n, :NB] = upper[n]
-        pltpu.make_async_copy(prod.at[n], out_ref.at[:, pl.ds(n * half, half)], local.at[6 + n]).start()
+    keep_tops = pltpu.make_async_copy(tops, tops_ref, local.at[12])
+    keep_tops.start()
     run(9)
-    for n in (0, 1):
-        pltpu.make_async_copy(prod.at[n], out_ref.at[:, pl.ds(n * half, half)], local.at[6 + n]).wait()
+    keep_tops.wait()
+    keep_sel.wait()
+    keep_panel.wait()
+    for i in range(4):
+        keep_upper(i).wait()
 
 
 def step(p_row, panel, matrix):
@@ -547,30 +553,80 @@
     return pl.pallas_call(
         step_kernel,
         out_shape=(
-            jax.ShapeDtypeStruct((rows, cols), F32),
+            jax.ShapeDtypeStruct((NB, cols), F32),
+            jax.ShapeDtypeStruct((NZ,) + panel.shape, F32),
+            jax.ShapeDtypeStruct((2, CAP, half), F32),
+            jax.ShapeDtypeStruct((CAP, rows), F32),
             jax.ShapeDtypeStruct((1,), F32),
         ),
         in_specs=[vm, vm, anyspec],
-        out_specs=(anyspec, pl.BlockSpec(memory_space=pltpu.SMEM)),
+        out_specs=(anyspec,) * 4 + (pl.BlockSpec(memory_space=pltpu.SMEM),),
         scratch_shapes=[
             v((rows, cols), F32), v((NZ,) + panel.shape, F32),
             v((2, NY, NX, CAP, half), F32), v((2, NY, NX, 4, 8, 128), F32),
             v((2, CAP, half), F32), v((NY, NX, 2, CAP, half), F32), v((NY - 1, CAP, half), F32),
             v((CAP, half), F32), v((2, CAP, half), F32), v((CAP, half), F32), v((8, 128), F32),
             v((8, NB), I32), v((3, NB, cols), BF16),
-            v((NB, NB), F32), v((4, 128, 128), F32), v((NB, CHIPS * CAP), BF16),
-            v((rows, NB), BF16), v((rows, NB), BF16), v((2, NB, half), F32), v((2, rows, half), F32),
+            v((64, NB), F32), v((NB, NB), F32), v((4, 128, 128), F32), v((NB, CHIPS * CAP), BF16),
+            v((NB, cols), F32), v((CAP, rows), F32),
             dma((2, NZ // 2, 2)), dma((2, NZ // 2, 2)),
             dma((2, NY // 2, 2)), dma((2, NY // 2, 2)),
             dma((2, NY // 2, 2)), dma((2, NY // 2, 2)),
             dma((NY,)), dma((NY,)), dma((NY,)), dma((NY,)),
-            dma((NZ,)), dma((4,)), dma((CHIPS,)), dma, dma((8,)),
+            dma((NZ,)), dma((4,)), dma((CHIPS,)), dma, dma((13,)),
             dma, dma, dma, dma, dma, dma, dma((CHIPS, 2)), dma, dma, dma,
             dma((2, 2)), dma, dma((NY - 1,)),
         ],
         compiler_params=pltpu.CompilerParams(collective_id=0, has_side_effects=True),
         name="step",
     )(p_row, panel, matrix)
+
+
+def update_kernel(me_ref, m_ref, p_ref, u_ref, tops_ref, sel_ref, out_ref, u_hi, u_lo):
+    i = pl.program_id(0)
+    half = tops_ref.shape[2]
+    block = out_ref.shape[0]
+
+    @pl.when(i == 0)
+    def _():
+        u = u_ref[...]
+        hi = u.astype(BF16)
+        u_hi[...] = hi
+        u_lo[...] = (u - hi.astype(F32)).astype(BF16)
+
+    p = p_ref[...]
+    p_hi = p.astype(BF16)
+    p_lo = (p - p_hi.astype(F32)).astype(BF16)
+    product = (mm(p_lo, u_hi[...]) + mm(p_hi, u_lo[...])) + mm(p_hi, u_hi[...])
+    sel = sel_ref[...].astype(BF16)
+    replaced = mm(sel, jnp.ones((CAP, 128), BF16), ((0,), (0,)))[:, :1] > 0.5
+    incoming = jnp.concatenate([select_rows(sel, tops_ref[n], ((0,), (0,))) for n in (0, 1)], axis=1)
+    out_ref[...] = jnp.where(replaced, incoming, m_ref[...]) - product
+
+    @pl.when((me_ref[0] == 0) & (i < NB // block))
+    def _():
+        out_ref[...] = u_ref[pl.ds(i * block, block)]
+
+
+def update(me, matrix, pall, upper, tops, sel):
+    rows, cols = matrix.shape
+    block = 256
+    whole = lambda shape: pl.BlockSpec(shape, lambda n: (0,) * len(shape))
+    return pl.pallas_call(
+        update_kernel,
+        grid=(rows // block,),
+        out_shape=jax.ShapeDtypeStruct(matrix.shape, F32),
+        in_specs=[
+            pl.BlockSpec(memory_space=pltpu.SMEM),
+            pl.BlockSpec((block, cols), lambda n: (n, 0)),
+            pl.BlockSpec((block, NB), lambda n: (n, 0)),
+            whole(upper.shape), whole(tops.shape),
+            pl.BlockSpec((CAP, block), lambda n: (0, n)),
+        ],
+        out_specs=pl.BlockSpec((block, cols), lambda n: (n, 0)),
+        scratch_shapes=[pltpu.VMEM((NB, cols), BF16), pltpu.VMEM((NB, cols), BF16)],
+        name="update",
+    )(me, matrix, pall.reshape(rows, NB), upper, tops, sel)
 
 
 def ring_sum(value, axis):
@@ -630,8 +686,11 @@
 
 
 def shards(matrix, panel, pivot_rows):
-    out, most = step(pivot_rows.reshape(1, NB), panel, matrix)
-    return lax.cond(most[0] < CAP, lambda: out, lambda: dense(matrix, panel, pivot_rows))
+    me = lax.axis_index("prow").reshape(1)
+    upper, pall, tops, sel, most = step(pivot_rows.reshape(1, NB), panel, matrix)
+    return lax.cond(most[0] < CAP,
+                    lambda: update(me, matrix, pall, upper, tops, sel),
+                    lambda: dense(matrix, panel, pivot_rows))
 
 
 def solution(mesh):

time: 74.6 us -> 71.9 us (0.964)
  the two profiles are of different devices: /device:TPU:1 before, /device:TPU:3 now
where the time goes in v3:
time: 71.9 us; the launch traced here: 71.7 us
  Pallas kernels  71.1 us (99%)
    pallas_call x1, Pallas kernels, step(): pl.pallas_call(step_kernel, out_shape=(jax.ShapeDtypeStruct((NB, cols), F...  64.3 us
    pallas_call x1, Pallas kernels, update(): pl.pallas_call(update_kernel, grid=(rows // block,), out_shape=jax.ShapeD...  6.76 us

profile of v3, /device:TPU:3, one launch (start us, length us, event | category | flops | bytes accessed | tf_op | source)
XLA Modules:
  0.0 71.7 jit_solution(12890189042538840720)
XLA Ops:
  0.0 0.0 copy-start.6
  0.0 0.0 copy-start.5
  0.0 64.3 %step.1 = (f32[512,768]{1,0:T(8,128)}, f32[12,64,512]{2,1,0:T(8,128)}, f32[2,32,384]{2,1,0:T(8,128)S(1)}, f32[32,768]{1,0:T(8,128)S(1)}, f32[1]{0:T(128)}) custom-call(s32[1,512]{1,0:T(1,128)} %bitcast.24, f32[64,512]{1,0:T(8,128)} %panel_ref.1, f32[768,768]{1,0:T(8,128)} %matrix_ref.1), custom_call_target="tpu_custom_call" | custom-call | tf_op jit(solution)/shard_map/step/pallas_call | solution.py:553
  64.9 0.0 copy-done.6
  64.9 0.0 copy-done.5
  64.9 6.8 %conditional.1 = (f32[768,768]{1,0:T(8,128)}) conditional(s32[]{:T(128)} %bitcast.8, (s32[512]{0:T(512)S(1)}, f32[768,768]{1,0:T(8,128)}, f32[64,512]{1,0:T(8,128)S(1)}) %tuple.75, (s32[]{:T(128)}, f32[12,64,512]{2,1,0:T(8,128)}, f32[768,768]{1,0:T(8,128)}, f32[512,768]{1,0:T(8,128)}, f32[2,32,384]{2,1,0:T(8,128)S(1)}, ...), branch_computations={%region_0.11_spmd, %region_11.12_spmd} | conditional | flops 13303746560 | bytes 176222848 | solution.py:691
  64.9 6.8 %update.1 = f32[768,768]{1,0:T(8,128)} custom-call(s32[1]{0:T(128)} %bitcast.5.me_ref, f32[768,768]{1,0:T(8,128)} %get-tuple-element.129.m_ref, f32[768,512]{1,0:T(8,128)} %bitcast.23, f32[512,768]{1,0:T(8,128)} %get-tuple-element.131.u_ref, f32[2,32,384]{2,1,0:T(8,128)S(1)} %get-tuple-element.132.tops_ref, f32[32,768]{1,0:T(8,128)S(1)} %get-tuple-element.133.sel_ref), custom_call_target="tpu_custom_call" | custom-call | tf_op jit(solution)/shard_map/cond/branch_1_fun/update/pallas_call | solution.py:615
Async XLA Ops:
  0.0 64.9 %copy-start.6 = (s32[512]{0:T(512)S(1)}, s32[512]{0:T(512)}, u32[]{:S(2)}) copy-start(s32[512]{0:T(512)} %param.13) | copy-start | bytes 6148
  0.0 64.9 %copy-start.5 = (f32[64,512]{1,0:T(8,128)S(1)}, f32[64,512]{1,0:T(8,128)}, u32[]{:S(2)}) copy-start(f32[64,512]{1,0:T(8,128)} %panel_ref.1) | copy-start | bytes 393220

commit v4 on v3

--- a/solution.py
+++ b/solution.py
@@ -351,7 +351,6 @@
                             for c in (0, 1):
                                 remote(staged.at[yy, xx, c], tops.at[c], top_send.at[q, c], top_recv,
                                        (q * 2 + c, z)).start()
-            zr.finish()
             lring.finish()
             remote(lows, lows, lpair_send, lpair_recv, partner).start()
             ref = slots_all.at[other]
@@ -371,6 +370,8 @@
             return remote(relay.at[i], tops.at[mine], rs_send.at[i], top_recv, dev(y=i + 1))
 
         def seg7():
+            zr.finish()
+
             @pl.when(relays)
             def _():
                 remote(relay, relay, rl_send.at[0, 0], rl_recv, partner).wait_recv()
@@ -502,8 +503,6 @@
     on_root(lambda: top_piece(3))
     run(4)
     run(5)
-    keep_panel = pltpu.make_async_copy(pall, p_ref, local.at[7])
-    keep_panel.start()
     for n in (0, 1):
         upper[:, n * half:n * half + half] = select_rows(
             perm[...], slots_all[n].reshape(CHIPS * CAP, half))
@@ -521,6 +520,8 @@
         off = jnp.where(i0 // 64 > i1 // 64, block, 0.0)
         inverse[k] = two - hdot(two, hdot(off, two))
     run(7)
+    keep_panel = pltpu.make_async_copy(pall, p_ref, local.at[7])
+    keep_panel.start()
 
     def keep_upper(i):
         return pltpu.make_async_copy(upper.at[pl.ds(128 * i, 128)], u_ref.at[pl.ds(128 * i, 128)],

time: 71.9 us -> 71.9 us (level)
  no operation moved by 1% of the time
where the time goes in v4:
time: 71.9 us; the launch traced here: 71.7 us
  Pallas kernels  71.1 us (99%)
    pallas_call x1, Pallas kernels, step(): pl.pallas_call(step_kernel, out_shape=(jax.ShapeDtypeStruct((NB, cols), F...  64.3 us
    pallas_call x1, Pallas kernels, update(): pl.pallas_call(update_kernel, grid=(rows // block,), out_shape=jax.ShapeD...  6.76 us

profile of v4, /device:TPU:3, one launch (start us, length us, event | category | flops | bytes accessed | tf_op | source)
XLA Modules:
  0.0 71.7 jit_solution(48118613532756192)
XLA Ops:
  0.0 0.0 copy-start.6
  0.0 0.0 copy-start.5
  0.0 64.3 %step.1 = (f32[512,768]{1,0:T(8,128)}, f32[12,64,512]{2,1,0:T(8,128)}, f32[2,32,384]{2,1,0:T(8,128)S(1)}, f32[32,768]{1,0:T(8,128)S(1)}, f32[1]{0:T(128)}) custom-call(s32[1,512]{1,0:T(1,128)} %bitcast.24, f32[64,512]{1,0:T(8,128)} %panel_ref.1, f32[768,768]{1,0:T(8,128)} %matrix_ref.1), custom_call_target="tpu_custom_call" | custom-call | tf_op jit(solution)/shard_map/step/pallas_call | solution.py:554
  64.9 0.0 copy-done.6
  64.9 0.0 copy-done.5
  64.9 6.8 %conditional.1 = (f32[768,768]{1,0:T(8,128)}) conditional(s32[]{:T(128)} %bitcast.8, (s32[512]{0:T(512)S(1)}, f32[768,768]{1,0:T(8,128)}, f32[64,512]{1,0:T(8,128)S(1)}) %tuple.75, (s32[]{:T(128)}, f32[12,64,512]{2,1,0:T(8,128)}, f32[768,768]{1,0:T(8,128)}, f32[512,768]{1,0:T(8,128)}, f32[2,32,384]{2,1,0:T(8,128)S(1)}, ...), branch_computations={%region_0.11_spmd, %region_11.12_spmd} | conditional | flops 13303746560 | bytes 176222848 | solution.py:692
  64.9 6.8 %update.1 = f32[768,768]{1,0:T(8,128)} custom-call(s32[1]{0:T(128)} %bitcast.5.me_ref, f32[768,768]{1,0:T(8,128)} %get-tuple-element.129.m_ref, f32[768,512]{1,0:T(8,128)} %bitcast.23, f32[512,768]{1,0:T(8,128)} %get-tuple-element.131.u_ref, f32[2,32,384]{2,1,0:T(8,128)S(1)} %get-tuple-element.132.tops_ref, f32[32,768]{1,0:T(8,128)S(1)} %get-tuple-element.133.sel_ref), custom_call_target="tpu_custom_call" | custom-call | tf_op jit(solution)/shard_map/cond/branch_1_fun/update/pallas_call | solution.py:616
Async XLA Ops:
  0.0 64.9 %copy-start.6 = (s32[512]{0:T(512)S(1)}, s32[512]{0:T(512)}, u32[]{:S(2)}) copy-start(s32[512]{0:T(512)} %param.13) | copy-start | bytes 6148
  0.0 64.9 %copy-start.5 = (f32[64,512]{1,0:T(8,128)S(1)}, f32[64,512]{1,0:T(8,128)}, u32[]{:S(2)}) copy-start(f32[64,512]{1,0:T(8,128)} %panel_ref.1) | copy-start | bytes 393220
